TPU v7x, 512 devices: a whole 4x8x8 slice. The times are simulated.
512 devices in a mesh: expert: 128 (over y, z, core), dp: 4 (over x).
Axes of the slice: x: 4, y: 8, z: 8, core: 2. Of those that a mesh axis runs over, the one named last changes fastest.
Arguments:
- hidden: bfloat16 [128, 4, 256, 1024], P('expert', 'dp'), may hold values from -6 to 6
- w_down: bfloat16 [128, 1024, 3584], P('expert', 'dp'), may hold values from -0.1875 to 0.1875
- expert_ids: int32 [4, 2048, 8], P('dp', 'expert'), may hold values from 0 to 127, all different within a row; in each aligned block of 16 rows (0 to 15, 16 to 31, ..., all dimensions but the last counted through in order) at most 2 rows name the same one
- route_weights: float32 [4, 2048, 8], P('dp', 'expert'), may hold values from 0.1 to 0.6
- grad_out: bfloat16 [4, 2048, 3584], P('dp', 'expert'), may hold values from -6 to 6
Outputs:
- mixed: bfloat16 [4, 2048, 3584], P('dp', 'expert')
- d_hidden: bfloat16 [128, 4, 256, 1024], P('expert', 'dp')
- d_w_down: bfloat16 [128, 1024, 3584], P('expert', 'dp')
- d_route: float32 [4, 2048, 8], P('dp', 'expert')
Inputs may be any that keep to these rules, and one draw needn't show every extreme that they name: `expert_ids`: among the 16 tokens of one device no expert is chosen more than 2 times, and some expert is chosen exactly 2 times; the 8 choices of a token are distinct.
All inputs are finite; a program needn't handle non-finite values.
Results may differ from a plain program's by a relative error of at most 0.0085.
Values may be sent and summed in bfloat16 or wider, within the bound.
A program may use at most 128 MiB of HBM per device.

v0:
```python
import jax
import jax.numpy as jnp
from jax import lax
from jax.sharding import PartitionSpec as P
from jax.experimental.layout import Layout, with_layout_constraint


def slot_ranks(choices, experts):
    flat = choices.reshape(-1)
    onehot = (flat[:, None] == jnp.arange(experts, dtype=jnp.int32)[None, :]).astype(jnp.int32)
    earlier = jnp.cumsum(onehot, axis=0) - onehot
    return jnp.sum(earlier * onehot, axis=1).reshape(choices.shape)


def on_device(hidden, w_down, expert_ids, route_weights, grad_out):
    experts = lax.axis_size("expert")
    groups = lax.axis_size("dp")
    slots = hidden.shape[2] // experts
    width = w_down.shape[2]
    w_whole = lax.all_gather(w_down, "dp", axis=1, tiled=True)[0]
    out_slots = jnp.dot(hidden[0, 0], w_whole, preferred_element_type=jnp.float32).astype(
        jnp.bfloat16
    )
    arrived = lax.all_to_all(
        out_slots.reshape(experts, slots, width), "expert", split_axis=0, concat_axis=0, tiled=True
    )
    arrived = arrived.reshape(experts * slots, width)
    choices = expert_ids[0]
    weights = route_weights[0]
    cotangent = grad_out[0].astype(jnp.float32)
    rows = choices * slots + slot_ranks(choices, experts)
    out_pair = arrived[rows].astype(jnp.float32)
    mixed = jnp.einsum("tk,tkd->td", weights, out_pair)
    d_route = jnp.einsum("td,tkd->tk", cotangent, out_pair)
    grad_pair = (weights[..., None] * cotangent[:, None, :]).astype(jnp.bfloat16)
    outgoing = jnp.zeros((experts * slots, width), jnp.bfloat16)
    outgoing = outgoing.at[rows.reshape(-1)].set(grad_pair.reshape(-1, width))
    mine = lax.all_to_all(
        outgoing.reshape(experts, 1, slots, width),
        "expert",
        split_axis=0,
        concat_axis=0,
        tiled=True,
    )
    own_grads = mine[:, 0]
    slot_grads = lax.all_gather(mine, "dp", axis=1, tiled=True)
    slot_grads = with_layout_constraint(slot_grads, Layout(major_to_minor=(1, 0, 2, 3)))
    d_hidden = jnp.einsum(
        "rd,hd->rh", own_grads.reshape(-1, width), w_whole, preferred_element_type=jnp.float32
    ).astype(jnp.bfloat16)
    columns = lax.all_to_all(hidden, "dp", split_axis=3, concat_axis=1, tiled=True)[0]
    columns = columns.reshape(groups, experts, slots, columns.shape[-1])
    d_weight = jnp.einsum(
        "gsch,sgcd->hd", columns, slot_grads, preferred_element_type=jnp.float32
    ).astype(jnp.bfloat16)
    d_weight = with_layout_constraint(d_weight, Layout(major_to_minor=(0, 1)))
    return (
        mixed.astype(jnp.bfloat16)[None],
        d_hidden.reshape(hidden.shape),
        d_weight[None],
        d_route[None],
    )


def solution(mesh):
    placed = (
        P("expert", "dp", None, None),
        P("expert", "dp", None),
        P("dp", "expert", None),
        P("dp", "expert", None),
        P("dp", "expert", None),
    )
    return jax.shard_map(
        on_device,
        mesh=mesh,
        in_specs=placed,
        out_specs=(
            P("dp", "expert", None),
            P("expert", "dp", None, None),
            P("expert", "dp", None),
            P("dp", "expert", None),
        ),
        check_vma=False,
    )
```

profile of v0, /device:TPU:1, one launch (start us, length us, event | category | flops | bytes accessed | tf_op | source)
XLA Modules:
  0.0 196.7 jit_solution(17713640946967735479)
XLA Ops:
  7.2 0.7 all-gather.3.cloned.1.call-update
  8.1 0.1 eq.15
  8.6 0.2 reduce_window_sum.11
  8.8 0.2 select_reduce_fusion
  9.0 2.5 %scatter_custom_fusion = bf16[256,3584]{1,0:T(8,128)(2,1)S(1)} fusion(s32[128]{0:T(128)S(1)} %fusion.39, f32[16,3584]{1,0:T(8,128)S(1)} %bitcast_convert_fusion.1, f32[128]{0:T(128)S(1)} %mul.53, bf16[]{:T(256)} %constant.7.clone.1), kind=kCustom, calls=%fused_computation.16 | custom fusion | flops 917504 | bytes 2064898 | tf_op jit(solution)/shard_map/scatter | solution.py:37
  11.5 1.6 reshape.99
  13.2 64.9 %all_to_all.25 = bf16[128,1,2,3584]{3,2,1,0:T(2,128)(2,1)S(1)} all-to-all(bf16[128,1,2,3584]{3,2,1,0:T(2,128)(2,1)} %reshape.99), channel_id=1, replica_groups=mesh['expert'=128,'dp'=4] {'expert'}, dimensions={0} | all-to-all | bytes 3670016 | tf_op jit(solution)/shard_map/all_to_all | solution.py:38
  78.1 1.4 copy.38
  79.5 1.0 copy-done
  80.5 0.8 copy.40
  81.4 0.5 broadcast.58
  81.9 3.8 %reduce = bf16[1024,256]{1,0:T(8,128)(2,1)S(1)} reduce(bf16[1024,1,1,256]{3,2,1,0:T(2,128)(2,1)S(1)} %bitcast.74, bf16[]{:T(256)} %broadcast.58), dimensions={1,2}, to_apply=%bitcast.67.reduce_sub_computation | reduce | bytes 1048578
  85.7 0.9 reshape.125
  86.6 4.0 %all-to-all-start.2 = ((bf16[4,2,32768]{2,1,0:T(2,128)(2,1)}), bf16[4,2,32768]{2,1,0:T(2,128)(2,1)S(1)}, u32[]{:S(2)}, u32[]{:S(2)}) async-start(bf16[4,2,32768]{2,1,0:T(2,128)(2,1)} %reshape.125), calls=%async_computation.2 | async-start | bytes 1048576 | tf_op jit(solution)/shard_map/all_to_all | solution.py:51
  90.7 4.8 %all-gather.3.cloned.1.call-done = bf16[1,1024,3584]{2,1,0:T(8,128)(2,1)} async-done(((bf16[1,256,3584]{2,1,0:T(8,128)(2,1)}), bf16[1,1024,3584]{2,1,0:T(8,128)(2,1)}) %all-gather.3.cloned.1.call-update) | async-done | bytes 7340048 | tf_op jit(solution)/shard_map/all_gather | solution.py:20
  95.5 6.4 %fusion.12 = bf16[256,3584]{1,0:T(8,128)(2,1)} fusion(bf16[1,1024,3584]{2,1,0:T(8,128)(2,1)} %all-gather.3.cloned.1.call-done, bf16[1,1,256,1024]{3,2,1,0:T(8,128)(2,1)S(1)} %copy-done.1), kind=kOutput, calls=%fused_computation.10 | convolution fusion | flops 1879965696 | bytes 9699328 | tf_op jit(solution)/shard_map/dot_general | solution.py:21
  101.9 4.7 %reshape.96 = bf16[128,2,3584]{2,1,0:T(2,128)(2,1)} reshape(bf16[256,3584]{1,0:T(8,128)(2,1)} %fusion.12) | data formatting | bytes 3670016 | tf_op jit(solution)/shard_map/reshape | solution.py:25
  106.6 20.3 %all-to-all-start = ((bf16[128,2,3584]{2,1,0:T(2,128)(2,1)}), bf16[128,2,3584]{2,1,0:T(2,128)(2,1)}, u32[]{:S(2)}, u32[]{:S(2)}) async-start(bf16[128,2,3584]{2,1,0:T(2,128)(2,1)} %reshape.96), calls=%async_computation | async-start | bytes 3670016 | tf_op jit(solution)/shard_map/all_to_all | solution.py:24
  127.1 0.1 reshape.103
  127.3 0.5 reshape.126
  128.0 0.3 copy.41
  128.3 1.6 reshape_squeeze.6
  129.9 6.6 %fusion.22 = bf16[1,1,256,1024]{3,2,1,0:T(8,128)(2,1)} fusion(bf16[256,3584]{1,0:T(8,128)(2,1)} %reshape_squeeze.6, bf16[1,1024,3584]{2,1,0:T(8,128)(2,1)} %all-gather.3.cloned.1.call-done), kind=kOutput, calls=%fused_computation.15 | convolution fusion | flops 1879310336 | bytes 9699328 | tf_op jit(solution)/shard_map/rd,hd->rh/dot_general | solution.py:48
  136.6 36.5 %all-to-all-done = bf16[128,2,3584]{2,1,0:T(2,128)(2,1)} async-done(((bf16[128,2,3584]{2,1,0:T(2,128)(2,1)}), bf16[128,2,3584]{2,1,0:T(2,128)(2,1)}, u32[]{:S(2)}, u32[]{:S(2)}) %all-to-all-start) | async-done | bytes 1835040 | tf_op jit(solution)/shard_map/all_to_all | solution.py:24
  173.1 4.1 %reshape.97 = bf16[256,3584]{1,0:T(8,128)(2,1)S(1)} reshape(bf16[128,2,3584]{2,1,0:T(2,128)(2,1)} %all-to-all-done) | data formatting | bytes 3670016 | tf_op jit(solution)/shard_map/reshape | solution.py:27
  177.2 1.1 gather_fusion
  178.3 0.4 fusion.27
  178.7 0.7 copy.66
  179.3 0.6 fusion.29
  179.9 0.7 copy.48
  180.6 2.8 %all-gather.5.cloned.1.call-done = bf16[128,4,2,3584]{3,0,2,1:T(8,128)(2,1)} async-done(((bf16[128,1,2,3584]{3,0,2,1:T(8,128)(2,1)}), bf16[128,4,2,3584]{3,0,2,1:T(8,128)(2,1)}) %all-gather.5.cloned.1.call-update) | async-done | bytes 7340048 | tf_op jit(solution)/shard_map/all_gather | solution.py:46
  183.4 6.4 %fusion.15 = bf16[1,256,3584]{2,1,0:T(8,128)(2,1)} fusion(bf16[128,4,2,3584]{3,0,2,1:T(8,128)(2,1)} %all-gather.5.cloned.1.call-done, bf16[4,128,2,256]{3,0,2,1:T(4,128)(2,1)S(1)} %bitcast.76), kind=kOutput, calls=%fused_computation.11 | convolution fusion | flops 1879965696 | bytes 9699328 | tf_op jit(solution)/shard_map/gsch,sgcd->hd/dot_general | solution.py:53
  (29 shorter events, 1.0 us)
Async XLA Ops:
  7.2 0.8 copy-start.3
  7.2 1.1 copy-start.4
  7.2 1.8 copy-start.2
  7.2 88.3 %all-gather.3.cloned.1.call-start = ((), (), s32[]{:S(2)}) async-start(), calls=%async_computation.3 | async-start | bytes 9175040 | tf_op jit(solution)/shard_map/all_gather | solution.py:20
  7.9 175.5 %all-gather.5.cloned.1.call-start = ((), (), s32[]{:S(2)}) async-start(), calls=%async_computation.4 | async-start | bytes 9175040 | tf_op jit(solution)/shard_map/all_gather | solution.py:46
  79.5 1.0 copy-start
  85.7 9.8 %copy-start.1 = (bf16[1,1,256,1024]{3,2,1,0:T(8,128)(2,1)S(1)}, bf16[1,1,256,1024]{3,2,1,0:T(8,128)(2,1)}, u32[]{:S(2)}) copy-start(bf16[1,1,256,1024]{3,2,1,0:T(8,128)(2,1)} %param.5) | copy-start | bytes 1572868
  86.6 20.0 %all-to-all-start.2 = ((bf16[4,2,32768]{2,1,0:T(2,128)(2,1)}), bf16[4,2,32768]{2,1,0:T(2,128)(2,1)S(1)}, u32[]{:S(2)}, u32[]{:S(2)}) async-start(bf16[4,2,32768]{2,1,0:T(2,128)(2,1)} %reshape.125), calls=%async_computation.2 | async-start | bytes 1048576 | tf_op jit(solution)/shard_map/all_to_all | solution.py:51
  106.6 66.5 %all-to-all-start = ((bf16[128,2,3584]{2,1,0:T(2,128)(2,1)}), bf16[128,2,3584]{2,1,0:T(2,128)(2,1)}, u32[]{:S(2)}, u32[]{:S(2)}) async-start(bf16[128,2,3584]{2,1,0:T(2,128)(2,1)} %reshape.96), calls=%async_computation | async-start | bytes 3670016 | tf_op jit(solution)/shard_map/all_to_all | solution.py:24
Sparse Core Ops, SparseCore 0:
  10.1 85.3 all-gather.2
  97.6 85.7 all-gather.4
where the time goes:
time: 197 us
  blocking collectives  64.9 us (33%)
  waiting for transfers between devices  44.9 us (23%)
  starting transfers between devices  24.4 us (12%)
  local copies, waits for them, and re-layouts  21.1 us (11%)
  matrix products  20.4 us (10%)
  between operations  14.2 us (7%)
  other arithmetic  6.83 us (3%)
    all_to_all x1, blocking collectives, on_device(): lax.all_to_all(outgoing.reshape(experts, 1, slots, width), 'expert', spli...  64.9 us
    all_to_all x1, waiting for transfers between devices, on_device(): lax.all_to_all(out_slots.reshape(experts, slots, width), 'expert', split_...  36.5 us
    all_to_all x1, starting transfers between devices, on_device(): lax.all_to_all(out_slots.reshape(experts, slots, width), 'expert', split_...  20.3 us
    dot_general x1, matrix products, on_device(): jnp.einsum('rd,hd->rh', own_grads.reshape(-1, width), w_whole, preferred_...  6.64 us
    dot_general x1, matrix products, on_device(): jnp.einsum('gsch,sgcd->hd', columns, slot_grads, preferred_element_type=j...  6.41 us
    dot_general x1, matrix products, on_device(): jnp.dot(hidden[0, 0], w_whole, preferred_element_type=jnp.float32)  6.37 us
    all_gather x1, waiting for transfers between devices, on_device(): w_whole = lax.all_gather(w_down, 'dp', axis=1, tiled=True)[0]  4.83 us
    reshape x1, local copies, waits for them, and re-layouts, on_device(): out_slots.reshape(experts, slots, width)  4.75 us
  transfers between devices with their start and end apart: 4, of which 3 were waited for; matrix products, arithmetic and copies ran while one was open for 21% of the time, Pallas kernels for 0%

commit v1 on v0

--- a/solution.py
+++ b/solution.py
@@ -1,8 +1,17 @@
+import functools
 import jax
 import jax.numpy as jnp
 from jax import lax
 from jax.sharding import PartitionSpec as P
 from jax.experimental.layout import Layout, with_layout_constraint
+
+
+def play_entries(t0, row_dim):
+    back = jnp.concatenate([t0] * jax.lax.axis_size("dp"), row_dim)
+    return jax.lax.all_to_all(back, "dp", row_dim, row_dim, tiled=True)
+
+
+close_sums_all = functools.partial(play_entries, row_dim=1)
 
 
 def slot_ranks(choices, experts):
@@ -17,7 +26,7 @@
     groups = lax.axis_size("dp")
     slots = hidden.shape[2] // experts
     width = w_down.shape[2]
-    w_whole = lax.all_gather(w_down, "dp", axis=1, tiled=True)[0]
+    w_whole = close_sums_all(w_down)[0]
     out_slots = jnp.dot(hidden[0, 0], w_whole, preferred_element_type=jnp.float32).astype(
         jnp.bfloat16
     )

time: 197 us -> 418 us (2.12)
  local copies, waits for them, and re-layouts: 21.1 us -> 123 us
  waiting for transfers between devices: 44.9 us -> 109 us
  other arithmetic: 6.83 us -> 61.5 us
  starting transfers between devices: 24.4 us -> 19.2 us
    concatenate x0 -> x1, local copies, waits for them, and re-layouts: none -> 80.7 us  [play_entries(): back = jnp.concatenate([t0] * jax.lax.axis_size('dp'), row_dim)]
    all_to_all x0 -> x1, waiting for transfers between devices: none -> 75.6 us  [play_entries(): return jax.lax.all_to_all(back, 'dp', row_dim, row_dim, tiled=True)]
    unnamed x1 -> x2, other arithmetic: 3.82 us -> 52.1 us
    unnamed x17 -> x21, local copies, waits for them, and re-layouts: 4.08 us -> 24.9 us
    all_to_all x1, starting transfers between devices: 20.3 us -> 9.92 us  [on_device(): lax.all_to_all(out_slots.reshape(experts, slots, width), 'expert', split_...]
    all_to_all x0 -> x1, starting transfers between devices: none -> 5.59 us  [play_entries(): return jax.lax.all_to_all(back, 'dp', row_dim, row_dim, tiled=True)]
    all_gather x1 -> x0, waiting for transfers between devices: 4.83 us -> none  [on_device(): w_whole = lax.all_gather(w_down, 'dp', axis=1, tiled=True)[0]]
    concatenate x0 -> x1, other arithmetic: none -> 4.78 us  [play_entries(): back = jnp.concatenate([t0] * jax.lax.axis_size('dp'), row_dim)]
  transfers between devices with their start and end apart: 4 -> 4, of which waited for: 3 -> 2; matrix products, arithmetic and copies ran while one was open for 21% -> 46% of each run, Pallas kernels for 0% -> 0%
where the time goes in v1:
time: 418 us; the launch traced here: 417 us
  local copies, waits for them, and re-layouts  123 us (29%)
  waiting for transfers between devices  109 us (26%)
  blocking collectives  64.9 us (16%)
  other arithmetic  61.5 us (15%)
  matrix products  24.5 us (6%)
  starting transfers between devices  19.2 us (5%)
  between operations  14.2 us (3%)
    concatenate x1, local copies, waits for them, and re-layouts, play_entries(): back = jnp.concatenate([t0] * jax.lax.axis_size('dp'), row_dim)  80.7 us
    all_to_all x1, waiting for transfers between devices, play_entries(): return jax.lax.all_to_all(back, 'dp', row_dim, row_dim, tiled=True)  75.6 us
    all_to_all x1, blocking collectives, on_device(): lax.all_to_all(outgoing.reshape(experts, 1, slots, width), 'expert', spli...  64.9 us
    unnamed x2, other arithmetic  52.1 us
    all_to_all x1, waiting for transfers between devices, on_device(): lax.all_to_all(out_slots.reshape(experts, slots, width), 'expert', split_...  33.7 us
    unnamed x21, local copies, waits for them, and re-layouts  24.9 us
    all_to_all x1, starting transfers between devices, on_device(): lax.all_to_all(out_slots.reshape(experts, slots, width), 'expert', split_...  9.92 us
    dot_general x1, matrix products, on_device(): jnp.einsum('rd,hd->rh', own_grads.reshape(-1, width), w_whole, preferred_...  8.63 us
  transfers between devices with their start and end apart: 4, of which 2 were waited for; matrix products, arithmetic and copies ran while one was open for 46% of the time, Pallas kernels for 0%

profile of v1, /device:TPU:1, one launch (start us, length us, event | category | flops | bytes accessed | tf_op | source)
XLA Modules:
  0.0 417.1 jit_solution(15471149811076187233)
XLA Ops:
  7.2 0.8 copy.53
  8.0 0.7 broadcast_multiply_fusion
  9.4 0.9 bitcast_convert_fusion.1
  10.3 0.8 copy.57
  11.1 2.5 scatter_custom_fusion
  13.7 1.6 reshape.99
  15.3 64.9 %all_to_all.30 = bf16[128,1,2,3584]{3,2,1,0:T(2,128)(2,1)S(1)} all-to-all(bf16[128,1,2,3584]{3,2,1,0:T(2,128)(2,1)} %reshape.99), channel_id=1, replica_groups=mesh['expert'=128,'dp'=4] {'expert'}, dimensions={0} | all-to-all | bytes 3670016 | tf_op jit(solution)/shard_map/all_to_all | solution.py:47
  80.2 1.4 copy.58
  81.7 4.8 %pad_maximum_fusion = bf16[1,1024,3584]{2,1,0:T(8,128)(2,1)S(1)} fusion(bf16[1,256,3584]{2,1,0:T(8,128)(2,1)} %param.6), kind=kLoop, calls=%fused_computation.2 | loop fusion | flops 29360128 | bytes 9175040 | tf_op jit(solution)/shard_map/concatenate | solution.py:10
  86.5 80.7 %copy.101 = bf16[1,1024,3584]{2,0,1:T(2,128)(2,1)} copy(bf16[1,1024,3584]{2,1,0:T(8,128)(2,1)S(1)} %pad_maximum_fusion) | data formatting | bytes 14680064 | tf_op jit(solution)/shard_map/concatenate | solution.py:10
  167.7 48.3 %reduce = bf16[1024,3584]{1,0:T(8,128)(2,1)} reduce(bf16[1024,1,3584]{2,1,0:T(2,128)(2,1)} %bitcast.81, bf16[]{:T(256)} %broadcast.58), dimensions={1}, to_apply=%bitcast.80.reduce_sub_computation | reduce | bytes 14680066
  215.9 9.0 %reshape.125 = bf16[4,2,458752]{2,1,0:T(2,128)(2,1)} reshape(bf16[1024,3584]{1,0:T(8,128)(2,1)} %reduce) | data formatting | bytes 14680064
  225.0 5.6 %all-to-all-start = ((bf16[4,2,458752]{2,1,0:T(2,128)(2,1)}), bf16[4,2,458752]{2,1,0:T(2,128)(2,1)}, u32[]{:S(2)}, u32[]{:S(2)}) async-start(bf16[4,2,458752]{2,1,0:T(2,128)(2,1)} %reshape.125), calls=%async_computation | async-start | bytes 14680064 | tf_op jit(solution)/shard_map/all_to_all | solution.py:11
  230.6 0.9 copy.60
  231.4 3.8 reduce.1
  235.3 0.9 reshape.127
  236.2 75.6 %all-to-all-done = bf16[4,2,458752]{2,1,0:T(2,128)(2,1)} async-done(((bf16[4,2,458752]{2,1,0:T(2,128)(2,1)}), bf16[4,2,458752]{2,1,0:T(2,128)(2,1)}, u32[]{:S(2)}, u32[]{:S(2)}) %all-to-all-start) | async-done | bytes 7340064 | tf_op jit(solution)/shard_map/all_to_all | solution.py:11
  311.8 3.7 all-to-all-start.3
  315.5 11.4 %reshape.126 = bf16[1024,1,3584]{2,1,0:T(2,128)(2,1)} reshape(bf16[4,2,458752]{2,1,0:T(2,128)(2,1)} %all-to-all-done) | data formatting | bytes 14680064
  326.9 8.5 %fusion.15 = bf16[256,3584]{1,0:T(8,128)(2,1)} fusion(bf16[1,1024,3584]{2,0,1:T(2,128)(2,1)} %bitcast.82, bf16[1,1,256,1024]{3,2,1,0:T(8,128)(2,1)S(1)} %copy-done.1), kind=kOutput, calls=%fused_computation.12 | convolution fusion | flops 1879965696 | bytes 9699328 | tf_op jit(solution)/shard_map/dot_general | solution.py:30
  335.4 4.8 %reshape.96 = bf16[128,2,3584]{2,1,0:T(2,128)(2,1)} reshape(bf16[256,3584]{1,0:T(8,128)(2,1)} %fusion.15) | data formatting | bytes 3670016 | tf_op jit(solution)/shard_map/reshape | solution.py:34
  340.2 9.9 %all-to-all-start.1 = ((bf16[128,2,3584]{2,1,0:T(2,128)(2,1)}), bf16[128,2,3584]{2,1,0:T(2,128)(2,1)}, u32[]{:S(2)}, u32[]{:S(2)}) async-start(bf16[128,2,3584]{2,1,0:T(2,128)(2,1)} %reshape.96), calls=%async_computation.1 | async-start | bytes 3670016 | tf_op jit(solution)/shard_map/all_to_all | solution.py:33
  351.2 1.1 copy.61
  352.3 1.6 reshape_squeeze.6
  353.9 8.6 %fusion.27 = bf16[1,1,256,1024]{3,2,1,0:T(8,128)(2,1)} fusion(bf16[256,3584]{1,0:T(8,128)(2,1)} %reshape_squeeze.6, bf16[1,1024,3584]{2,0,1:T(2,128)(2,1)} %bitcast.83), kind=kOutput, calls=%fused_computation.19 | convolution fusion | flops 1879310336 | bytes 9699328 | tf_op jit(solution)/shard_map/rd,hd->rh/dot_general | solution.py:57
  362.6 33.7 %all-to-all-done.1 = bf16[128,2,3584]{2,1,0:T(2,128)(2,1)} async-done(((bf16[128,2,3584]{2,1,0:T(2,128)(2,1)}), bf16[128,2,3584]{2,1,0:T(2,128)(2,1)}, u32[]{:S(2)}, u32[]{:S(2)}) %all-to-all-start.1) | async-done | bytes 1835040 | tf_op jit(solution)/shard_map/all_to_all | solution.py:33
  396.3 4.1 reshape.97
  400.3 1.1 gather_fusion
  401.9 0.7 copy.100
  402.5 0.6 fusion.34
  403.1 0.7 copy.68
  403.8 6.4 %fusion.18 = bf16[1,256,3584]{2,1,0:T(8,128)(2,1)} fusion(bf16[128,4,2,3584]{3,0,2,1:T(8,128)(2,1)} %all-gather.2.cloned.1.call-done, bf16[4,128,2,256]{3,0,2,1:T(4,128)(2,1)S(1)} %bitcast.87), kind=kOutput, calls=%fused_computation.13 | convolution fusion | flops 1879965696 | bytes 9699328 | tf_op jit(solution)/shard_map/gsch,sgcd->hd/dot_general | solution.py:62
  (35 shorter events, 2.8 us)
Async XLA Ops:
  7.2 396.6 %all-gather.2.cloned.1.call-start = ((), (), s32[]{:S(2)}) async-start(), calls=%async_computation.4 | async-start | bytes 9175040 | tf_op jit(solution)/shard_map/all_gather | solution.py:55
  225.0 5.6 %copy-start = (bf16[1,1,256,1024]{3,2,1,0:T(8,128)(2,1)S(1)}, bf16[1,1,256,1024]{3,2,1,0:T(8,128)(2,1)}, u32[]{:S(2)}) copy-start(bf16[1,1,256,1024]{3,2,1,0:T(8,128)(2,1)} %param.5) | copy-start | bytes 1572868
  225.0 86.8 %all-to-all-start = ((bf16[4,2,458752]{2,1,0:T(2,128)(2,1)}), bf16[4,2,458752]{2,1,0:T(2,128)(2,1)}, u32[]{:S(2)}, u32[]{:S(2)}) async-start(bf16[4,2,458752]{2,1,0:T(2,128)(2,1)} %reshape.125), calls=%async_computation | async-start | bytes 14680064 | tf_op jit(solution)/shard_map/all_to_all | solution.py:11
  311.8 28.4 %all-to-all-start.3 = ((bf16[4,2,32768]{2,1,0:T(2,128)(2,1)}), bf16[4,2,32768]{2,1,0:T(2,128)(2,1)S(1)}, u32[]{:S(2)}, u32[]{:S(2)}) async-start(bf16[4,2,32768]{2,1,0:T(2,128)(2,1)} %reshape.127), calls=%async_computation.3 | async-start | bytes 1048576 | tf_op jit(solution)/shard_map/all_to_all | solution.py:60
  315.5 11.4 %copy-start.1 = (bf16[1,1,256,1024]{3,2,1,0:T(8,128)(2,1)S(1)}, bf16[1,1,256,1024]{3,2,1,0:T(8,128)(2,1)}, u32[]{:S(2)}) copy-start(bf16[1,1,256,1024]{3,2,1,0:T(8,128)(2,1)} %param.5) | copy-start | bytes 1572868
  326.9 23.4 %copy-start.4 = (s32[1,16,8]{1,2,0:T(8,128)S(1)}, s32[1,16,8]{1,2,0:T(8,128)}, u32[]{:S(2)}) copy-start(s32[1,16,8]{1,2,0:T(8,128)} %param.7) | copy-start | bytes 1540
  326.9 23.6 %copy-start.5 = (f32[1,16,8]{1,2,0:T(8,128)S(1)}, f32[1,16,8]{1,2,0:T(8,128)}, u32[]{:S(2)}) copy-start(f32[1,16,8]{1,2,0:T(8,128)} %param.8) | copy-start | bytes 1540
  340.2 56.1 %all-to-all-start.1 = ((bf16[128,2,3584]{2,1,0:T(2,128)(2,1)}), bf16[128,2,3584]{2,1,0:T(2,128)(2,1)}, u32[]{:S(2)}, u32[]{:S(2)}) async-start(bf16[128,2,3584]{2,1,0:T(2,128)(2,1)} %reshape.96), calls=%async_computation.1 | async-start | bytes 3670016 | tf_op jit(solution)/shard_map/all_to_all | solution.py:33
  362.6 40.0 %copy-start.3 = (bf16[1,16,3584]{2,1,0:T(8,128)(2,1)S(1)}, bf16[1,16,3584]{2,1,0:T(8,128)(2,1)}, u32[]{:S(2)}) copy-start(bf16[1,16,3584]{2,1,0:T(8,128)(2,1)} %param.9) | copy-start | bytes 344068
  362.6 41.2 %copy-start.2 = (bf16[1,4,1,256,256]{4,1,3,2,0:T(4,128)(2,1)S(1)}, bf16[1,4,1,256,256]{4,1,3,2,0:T(4,128)(2,1)}, u32[]{:S(2)}) copy-start(bf16[1,4,1,256,256]{4,1,3,2,0:T(4,128)(2,1)} %copy.61) | copy-start | bytes 1572868
Sparse Core Ops, SparseCore 0:
  81.8 74.3 all-gather.1
